TPU v7x, 128 devices: a whole 4x4x4 slice. The times are simulated.
128 devices in a mesh: pb: 8 (over z_hi, x), ka: 16 (over z_lo, y, core).
Axes of the slice: x: 4, y: 4, z: 4 (z_hi: 2, z_lo: 2; z = z_hi * 2 + z_lo), core: 2. Of those that a mesh axis runs over, the one named last changes fastest.
Arguments:
- feat_first: bfloat16 [32768, 128], P(('pb', 'ka')), may hold values from -16 to 16
- feat_second: bfloat16 [32768, 128], P(('ka', 'pb')), may hold values from -18 to 18
- value_weight: bfloat16 [128, 128], replicated, may hold values from -0.5 to 0.5
- out_weight: bfloat16 [128, 128], replicated, may hold values from -0.5 to 0.5
- conv_weight: bfloat16 [3, 3, 128, 128], replicated, may hold values from -0.1875 to 0.1875
- conv_bias: bfloat16 [128], replicated, may hold values from -3 to 3
Outputs:
- refined: bfloat16 [128, 256, 128], P(('pb', 'ka'))
All inputs are finite; a program needn't handle non-finite values.
Results may differ from a plain program's by a relative error of at most 0.0055.
Values may be sent and summed in bfloat16 or wider, within the bound.
No kernel may reach another device: no remote copies, remote signals or barrier semaphores. Data moves between devices by JAX's collectives and lax.ppermute only.
A program may use at most 192 MiB of HBM per device.

v0:
```python
import jax
import jax.numpy as jnp
from jax import lax
from jax.sharding import PartitionSpec as P

WIMG = 256


floor_score = -1e30


def joined(value, axis, join):
    pieces = jax.tree.map(lambda part: lax.all_gather(part, axis), value)
    head = jax.tree.map(lambda part: part[0], pieces)
    tail = jax.tree.map(lambda part: part[1:], pieces)
    subtotal, _ = lax.scan(lambda subtotal, share: (join(subtotal, share), None), head, tail)
    return subtotal


def padded_2(block, sides, width):
    for axis, dim in sides:
        count = lax.axis_size(axis)
        forward = [(i, i + 1) for i in range(count - 1)]
        backward = [(target, source) for source, target in forward]
        low = lax.ppermute(
            lax.slice_in_dim(block, block.shape[dim] - width, None, axis=dim), axis, forward
        )
        high = lax.ppermute(lax.slice_in_dim(block, 0, width, axis=dim), axis, backward)
        block = jnp.concatenate([low, block, high], axis=dim)
    return block


def combine_parts(earlier, later):
    new_peak = jnp.maximum(earlier[0], later[0])
    early_factor = jnp.exp(earlier[0] - new_peak)
    late_factor = jnp.exp(later[0] - new_peak)
    new_mass = earlier[1] * early_factor + later[1] * late_factor
    new_weighted = earlier[2] * early_factor[:, None] + later[2] * late_factor[:, None]
    return (new_peak, new_mass, new_weighted)


def refine(padded, center, conv_weight, conv_bias):
    num_rows, num_cols, channels = center.shape
    accum_sum = jnp.zeros((num_rows * num_cols, channels), jnp.float32)
    for row_shift in range(3):
        for col_shift in range(3):
            window = padded[
                row_shift : row_shift + num_rows, col_shift : col_shift + num_cols
            ].reshape(num_rows * num_cols, channels)
            accum_sum = accum_sum + jnp.dot(
                window, conv_weight[row_shift, col_shift], preferred_element_type=jnp.float32
            )
    conv_out = accum_sum.reshape(num_rows, num_cols, channels) + conv_bias.astype(jnp.float32)
    return (center.astype(jnp.float32) + jax.nn.gelu(conv_out)).astype(jnp.bfloat16)


def local(feat_first, feat_second, value_weight, out_weight, conv_weight, conv_bias):
    own_rows, feat_width = feat_first.shape
    score_scale = feat_width ** (-0.5)
    values = jnp.dot(feat_second, value_weight, preferred_element_type=jnp.float32).astype(
        jnp.bfloat16
    )
    queries = lax.all_gather(feat_first, "ka", axis=0, tiled=True)
    total_rows = queries.shape[0]
    block_rows = min(1024, total_rows)
    num_blocks = total_rows // block_rows
    query_blocks = queries.reshape(num_blocks, block_rows, feat_width)
    start_carry = (
        jnp.full((num_blocks, block_rows), floor_score, jnp.float32),
        jnp.zeros((num_blocks, block_rows), jnp.float32),
        jnp.zeros((num_blocks, block_rows, feat_width), jnp.float32),
    )
    keys_part = lax.all_gather(feat_second, "pb", axis=0, tiled=True)
    values_part = lax.all_gather(values, "pb", axis=0, tiled=True)

    def update(members):
        query_block, old_peak, old_mass, old_weighted = members
        scores = (
            jnp.einsum("qc,kc->qk", query_block, keys_part, preferred_element_type=jnp.float32)
            * score_scale
        )
        new_peak = jnp.maximum(old_peak, jnp.max(scores, axis=1))
        expo = jnp.exp(scores - new_peak[:, None])
        decay_factor = jnp.exp(old_peak - new_peak)
        new_mass = old_mass * decay_factor + jnp.sum(expo, axis=1)
        new_weighted = old_weighted * decay_factor[:, None] + jnp.dot(
            expo.astype(jnp.bfloat16), values_part, preferred_element_type=jnp.float32
        )
        return (new_peak, new_mass, new_weighted)

    row_peak, row_mass, weighted = lax.map(update, (query_blocks,) + tuple(start_carry))
    row_peak = row_peak.reshape(total_rows)
    row_mass = row_mass.reshape(total_rows)
    weighted = weighted.reshape(total_rows, feat_width)
    own_start = lax.axis_index("ka") * own_rows
    merged = joined((row_peak, row_mass, weighted), "ka", combine_parts)
    mass_own = lax.dynamic_slice_in_dim(merged[1], own_start, own_rows, 0)
    weighted_own = lax.dynamic_slice_in_dim(merged[2], own_start, own_rows, 0)
    message = (weighted_own / mass_own[:, None]).astype(jnp.bfloat16)
    mixed_rows = (
        feat_first.astype(jnp.float32)
        + jnp.dot(message, out_weight, preferred_element_type=jnp.float32)
    ).astype(jnp.bfloat16)
    strip_rows = own_rows // WIMG
    strip_image = mixed_rows.reshape(strip_rows, WIMG, feat_width)
    tile_image = lax.all_to_all(strip_image, "ka", split_axis=1, concat_axis=0, tiled=True)
    padded = padded_2(tile_image, (("pb", 0), ("ka", 1)), 1)
    result = refine(padded, tile_image, conv_weight, conv_bias)
    refined = lax.all_to_all(result, "ka", split_axis=0, concat_axis=1, tiled=True)
    return refined


def solution(mesh):
    in_specs = (P(("pb", "ka"), None), P(("ka", "pb"), None), P(), P(), P(), P())
    out_specs = P(("pb", "ka"), None, None)
    return jax.shard_map(local, mesh=mesh, in_specs=in_specs, out_specs=out_specs, check_vma=False)
```

profile of v0, /device:TPU:6, one launch (start us, length us, event | category | flops | bytes accessed | tf_op | source)
XLA Modules:
  0.0 423.7 jit_solution(18136325351554592396)
XLA Ops:
  8.3 35.4 %all_gather.19 = bf16[2048,128]{1,0:T(8,128)(2,1)S(1)} all-gather(bf16[256,128]{1,0:T(8,128)(2,1)} %param.11), channel_id=1, replica_groups=mesh['pb'=8,'ka'=16] {'pb'}, dimensions={0}, use_global_device_ids=true | all-gather | bytes 589824 | tf_op jit(solution)/shard_map/all_gather | solution.py:73
  43.7 35.0 %all_gather.20 = bf16[2048,128]{1,0:T(8,128)(2,1)S(1)} all-gather(bf16[256,128]{1,0:T(8,128)(2,1)S(1)} %convolution_convert_fusion), channel_id=1, replica_groups=mesh['pb'=8,'ka'=16] {'pb'}, dimensions={0}, use_global_device_ids=true | all-gather | bytes 589824 | tf_op jit(solution)/shard_map/all_gather | solution.py:74
  78.7 28.9 %while.28 = (s32[]{:T(128)}, f32[4,1024]{1,0:T(4,128)S(1)}, f32[4,1024]{1,0:T(4,128)S(1)}, f32[4,1024,128]{2,1,0:T(8,128)}, bf16[4,1024,128]{2,1,0:T(8,128)(2,1)...) while((s32[]{:T(128)}, f32[4,1024]{1,0:T(4,128)S(1)}, ...), condition=%wide.region_3.4_spmd, body=%wide.region_0.3_spmd.sunk | while | flops 1090654208 | bytes 27063396 | solution.py:91
  107.7 21.2 %all-gather = f32[16,1,4096]{2,1,0:T(1,128)S(1)} all-gather(f32[1,1,4096]{2,1,0:T(1,128)S(1)} %reshape.97), channel_id=1, replica_groups=mesh['pb'=8,'ka'=16] {'ka'}, dimensions={0}, use_global_device_ids=true | all-gather | bytes 278528 | tf_op jit(solution)/shard_map/all_gather | solution.py:13
  128.9 17.3 %all-gather.1 = f32[16,1,4096]{2,1,0:T(1,128)S(1)} all-gather(f32[1,1,4096]{2,1,0:T(1,128)S(1)} %reshape.99), channel_id=1, replica_groups=mesh['pb'=8,'ka'=16] {'ka'}, dimensions={0}, use_global_device_ids=true | all-gather | bytes 278528 | tf_op jit(solution)/shard_map/all_gather | solution.py:13
  146.6 135.9 %all-gather.7.cloned.1.call-done = f32[16,4096,128]{2,1,0:T(8,128)} async-done(((f32[1,4096,128]{2,1,0:T(8,128)}), f32[16,4096,128]{2,1,0:T(8,128)}) %all-gather.7.cloned.1.call-update) | async-done | bytes 33554448 | tf_op jit(solution)/shard_map/all_gather | solution.py:13
  282.5 21.8 %slice.127 = f32[15,4096,128]{2,1,0:T(8,128)} slice(f32[16,4096,128]{2,1,0:T(8,128)} %all-gather.7.cloned.1.call-done), slice={[1:16], [0:4096], [0:128]} | slice | bytes 62914560 | tf_op jit(solution)/shard_map/slice | solution.py:15
  306.0 63.9 %while.29 = (s32[]{:T(128)}, f32[4096]{0:T(1024)S(1)}, f32[4096]{0:T(1024)S(1)}, f32[4096,128]{1,0:T(8,128)S(1)}, f32[15,4096]{1,0:T(8,128)S(1)}, /*index=5*/f32...) while((s32[]{:T(128)}, f32[4096]{0:T(1024)S(1)}, f32[4096]{0:T(1024)S(1)}, f32[4096,128]{1,0:T(8,128)S(1)}, ...), condition=%wide.region_5.6_spmd, body=%wide.region_4.5_spmd.sunk | while | flops 1597442 | bytes 6520925 | solution.py:16
  306.1 4.2 fusion.81
  310.4 4.2 fusion.81
  314.6 4.2 fusion.81
  318.9 4.2 fusion.81
  323.1 4.2 fusion.81
  327.4 4.2 fusion.81
  331.7 4.2 fusion.81
  335.9 4.2 fusion.81
  340.2 4.2 fusion.81
  357.2 4.2 fusion.81
  361.4 4.2 fusion.81
  365.7 4.2 fusion.81
  371.9 10.1 %all_to_all.24 = bf16[16,2,1024]{2,1,0:T(2,128)(2,1)S(1)} all-to-all(bf16[16,2,1024]{2,1,0:T(2,128)(2,1)S(1)} %reshape.109), channel_id=1, replica_groups=mesh['pb'=8,'ka'=16] {'ka'}, dimensions={0} | all-to-all | bytes 131072 | tf_op jit(solution)/shard_map/all_to_all | solution.py:106
  382.0 4.9 %collective-permute-start = (bf16[1,16,128]{2,1,0:T(8,128)(2,1)S(1)}, bf16[1,16,128]{2,1,0:T(8,128)(2,1)S(1)}, u32[]{:S(2)}, u32[]{:S(2)}) collective-permute-start(bf16[1,16,128]{2,1,0:T(8,128)(2,1)S(1)} %copy.19), channel_id=1, source_target_pairs={{0,16},{16,32},{32,48},{48,64},{64,80},{80,96},{96,112},{1,17},{17... | collective-permute-start | bytes 12296 | tf_op jit(solution)/shard_map/ppermute | solution.py:25
  388.9 7.1 %collective-permute-done.1 = bf16[1,16,128]{2,1,0:T(8,128)(2,1)S(1)} collective-permute-done((bf16[1,16,128]{2,1,0:T(8,128)(2,1)S(1)}, bf16[1,16,128]{2,1,0:T(8,128)(2,1)S(1)}, u32[]{:S(2)}, u32[]{:S(2)}) %collective-permute-start.1) | collective-permute-done | bytes 4128 | tf_op jit(solution)/shard_map/ppermute | solution.py:28
  402.6 13.6 %all_to_all.25 = bf16[16,16,128]{2,1,0:T(8,128)(2,1)S(1)} all-to-all(bf16[16,16,128]{2,1,0:T(8,128)(2,1)S(1)} %fusion.30), channel_id=1, replica_groups=mesh['pb'=8,'ka'=16] {'ka'}, dimensions={0} | all-to-all | bytes 131072 | tf_op jit(solution)/shard_map/all_to_all | solution.py:109
  (124 shorter events, 57.1 us)
Async XLA Ops:
  6.5 0.8 copy-start
  6.5 72.1 %all-gather.5.cloned.1.call-start = ((), (), s32[]{:S(2)}) async-start(), calls=%async_computation.2 | async-start | bytes 1114112 | tf_op jit(solution)/shard_map/all_gather | solution.py:63
  7.3 275.2 %all-gather.7.cloned.1.call-start = ((), (), s32[]{:S(2)}) async-start(), calls=%async_computation.3 | async-start | bytes 35651584 | tf_op jit(solution)/shard_map/all_gather | solution.py:13
  306.0 64.0 %copy-start.3 = (bf16[256,128]{1,0:T(8,128)(2,1)S(1)}, bf16[256,128]{1,0:T(8,128)(2,1)}, u32[]{:S(2)}) copy-start(bf16[256,128]{1,0:T(8,128)(2,1)} %param.10) | copy-start | bytes 196612
  306.0 64.0 %copy-start.4 = (bf16[128,128]{1,0:T(8,128)(2,1)S(1)}, bf16[128,128]{1,0:T(8,128)(2,1)}, u32[]{:S(2)}) copy-start(bf16[128,128]{1,0:T(8,128)(2,1)} %param.13) | copy-start | bytes 98308
  306.0 82.9 %copy-start.5 = (bf16[128]{0:T(256)(128)(2,1)S(1)}, bf16[128]{0:T(256)(128)(2,1)}, u32[]{:S(2)}) copy-start(bf16[128]{0:T(256)(128)(2,1)} %param.15) | copy-start | bytes 772
  306.0 92.7 %copy-start.2 = (bf16[3,3,128,128]{3,2,1,0:T(8,128)(2,1)S(1)}, bf16[3,3,128,128]{3,2,1,0:T(8,128)(2,1)}, u32[]{:S(2)}) copy-start(bf16[3,3,128,128]{3,2,1,0:T(8,128)(2,1)} %param.14) | copy-start | bytes 884740
  369.9 47.0 %copy-start.1 = (bf16[128,128]{1,0:T(8,128)(2,1)S(1)}, bf16[128,128]{1,0:T(8,128)(2,1)}, u32[]{:S(2)}) copy-start(bf16[128,128]{1,0:T(8,128)(2,1)} %param.12) | copy-start | bytes 98308
  382.0 6.8 %collective-permute-start = (bf16[1,16,128]{2,1,0:T(8,128)(2,1)S(1)}, bf16[1,16,128]{2,1,0:T(8,128)(2,1)S(1)}, u32[]{:S(2)}, u32[]{:S(2)}) collective-permute-start(bf16[1,16,128]{2,1,0:T(8,128)(2,1)S(1)} %copy.19), channel_id=1, source_target_pairs={{0,16},{16,32},{32,48},{48,64},{64,80},{80,96},{96,112},{1,17},{17... | collective-permute-start | bytes 12296 | tf_op jit(solution)/shard_map/ppermute | solution.py:25
  386.9 9.1 %collective-permute-start.1 = (bf16[1,16,128]{2,1,0:T(8,128)(2,1)S(1)}, bf16[1,16,128]{2,1,0:T(8,128)(2,1)S(1)}, u32[]{:S(2)}, u32[]{:S(2)}) collective-permute-start(bf16[1,16,128]{2,1,0:T(8,128)(2,1)S(1)} %copy.20), channel_id=1, source_target_pairs={{16,0},{32,16},{48,32},{64,48},{80,64},{96,80},{112,96},{17,1},{33... | collective-permute-start | bytes 12296 | tf_op jit(solution)/shard_map/ppermute | solution.py:28
  396.0 2.8 collective-permute-start.2
  397.3 3.9 collective-permute-start.3
Sparse Core Ops, SparseCore 0:
  9.0 34.7 all-gather.4
  107.8 174.6 all-gather.6
where the time goes:
time: 426 us; the launch traced here: 424 us
  waiting for transfers between devices  146 us (34%)
  blocking collectives  132 us (31%)
  other arithmetic  71.8 us (17%)
  local copies, waits for them, and re-layouts  26.5 us (6%)
  matrix products  23 us (5%)
  between operations  13.8 us (3%)
  starting transfers between devices  9.4 us (2%)
    all_gather x1, waiting for transfers between devices, joined(): pieces = jax.tree.map(lambda part: lax.all_gather(part, axis), value)  136 us
    add x15, other arithmetic, combine_parts(): earlier[2] * early_factor[:, None] + later[2] * late_factor[:, None]  62.5 us
    all_gather x2, blocking collectives, joined(): pieces = jax.tree.map(lambda part: lax.all_gather(part, axis), value)  38.5 us
    all_gather x1, blocking collectives, local(): keys_part = lax.all_gather(feat_second, 'pb', axis=0, tiled=True)  35.4 us
    all_gather x1, blocking collectives, local(): values_part = lax.all_gather(values, 'pb', axis=0, tiled=True)  35 us
    slice x3, local copies, waits for them, and re-layouts, joined(): tail = jax.tree.map(lambda part: part[1:], pieces)  21.8 us
    all_to_all x1, blocking collectives, local(): lax.all_to_all(result, 'ka', split_axis=0, concat_axis=1, tiled=True)  13.6 us
    dot_general x4, matrix products, update(): jnp.dot(expo.astype(jnp.bfloat16), values_part, preferred_element_type=jn...  11.4 us
  transfers between devices with their start and end apart: 6, of which 3 were waited for; matrix products, arithmetic and copies ran while one was open for 0% of the time, Pallas kernels for 0%

commit v1 on v0

v1 whole, which is shorter than its diff:
```python
import functools

import jax
import jax.numpy as jnp
from jax import lax
from jax.experimental import pallas as pl
from jax.experimental.pallas import tpu as pltpu
from jax.sharding import PartitionSpec as P

AXES = ("pb", "ka")
SIZES = dict(zh=2, x=4, zl=2, y=4, c=2)
LOG2E = 1.4426950408889634
VMEM = pl.BlockSpec(memory_space=pltpu.VMEM)
NT = (((1,), (1,)), ((), ()))


def place(index):
    at = {}
    for name in reversed(SIZES):
        index, at[name] = divmod(index, SIZES[name])
    at["z"] = at["zh"] * 2 + at["zl"]
    return at


def number(at):
    index = 0
    for name, size in SIZES.items():
        index = index * size + at[name]
    return index


def send(block, **shift):
    pairs = []
    for source in range(128):
        at = place(source)
        for name, step in shift.items():
            size = 4 if name == "z" else SIZES[name]
            at[name] = (at[name] + step) % size
        if "z" in shift:
            at["zh"], at["zl"] = divmod(at["z"], 2)
        pairs.append((source, number(at)))
    return lax.ppermute(block, AXES, pairs)


def params():
    return pltpu.CompilerParams(vmem_limit_bytes=48 << 20)


def attend(q, pieces, scale, start=None, chunk=512):
    peak, weighted = (None, None) if start is None else start
    ones = jnp.ones((chunk, 128), jnp.bfloat16)
    for keys_ref, values_ref in pieces:
        for at in range(0, keys_ref.shape[0], chunk):
            k = keys_ref[at : at + chunk]
            v = jnp.concatenate([values_ref[at : at + chunk], ones], axis=1)
            s = lax.dot_general(q, k, NT, preferred_element_type=jnp.float32)
            high = jnp.max(s, axis=1, keepdims=True)
            new = high if peak is None else jnp.maximum(peak, high)
            p = jnp.exp2(((s - new) * scale).astype(jnp.bfloat16))
            part = jnp.dot(p, v, preferred_element_type=jnp.float32)
            weighted = part if peak is None else weighted * jnp.exp2((peak - new) * scale) + part
            peak = new
    return peak, weighted


def project(vw, pieces, val_refs):
    out = []
    for keys_ref, val_ref in zip(pieces, val_refs):
        val_ref[...] = jnp.dot(
            keys_ref[...], vw[...], preferred_element_type=jnp.float32
        ).astype(jnp.bfloat16)
        out.append((keys_ref, val_ref))
    return out


def first_kernel(scale, nq, nk, *refs):
    q_refs, k_refs = refs[:nq], refs[nq : nq + nk]
    vw = refs[nq + nk]
    outs = refs[nq + nk + 1 : nq + nk + 1 + 2 * nq]
    vals = refs[nq + nk + 1 + 2 * nq :]
    pieces = project(vw, k_refs, vals)
    for i in range(nq):
        peak, weighted = attend(q_refs[i][...], pieces, scale)
        outs[2 * i][...] = jnp.broadcast_to(peak, (256, 128))
        outs[2 * i + 1][...] = weighted


def first_call(queries, pieces, vw, scale):
    nq, nk = len(queries), len(pieces)
    shapes = []
    for _ in range(nq):
        shapes += [
            jax.ShapeDtypeStruct((256, 128), jnp.float32),
            jax.ShapeDtypeStruct((256, 256), jnp.float32),
        ]
    out = pl.pallas_call(
        functools.partial(first_kernel, scale, nq, nk),
        out_shape=shapes,
        in_specs=[VMEM] * (nq + nk + 1),
        out_specs=[VMEM] * (2 * nq),
        scratch_shapes=[pltpu.VMEM(p.shape, jnp.bfloat16) for p in pieces],
        compiler_params=params(),
        name="first_keys",
    )(*queries, *pieces, vw)
    return [(out[2 * i], out[2 * i + 1]) for i in range(nq)]


def values_kernel(nk, *refs):
    project(refs[nk], refs[:nk], refs[nk + 1 :])


def values_call(pieces, vw):
    return pl.pallas_call(
        functools.partial(values_kernel, len(pieces)),
        out_shape=[jax.ShapeDtypeStruct(p.shape, jnp.bfloat16) for p in pieces],
        in_specs=[VMEM] * (len(pieces) + 1),
        out_specs=[VMEM] * len(pieces),
        compiler_params=params(),
        name="values",
    )(*pieces, vw)


def split3(x):
    high = x.astype(jnp.bfloat16)
    rest = x - high.astype(jnp.float32)
    mid = rest.astype(jnp.bfloat16)
    low = (rest - mid.astype(jnp.float32)).astype(jnp.bfloat16)
    return high.astype(jnp.float32), mid.astype(jnp.float32), low.astype(jnp.float32)


def pack(peak, weighted, scale, out_ref):
    mass = weighted[:, 128:]
    out_ref[0:256] = (weighted[:, :128] / mass).astype(jnp.bfloat16)
    level = peak * scale + jnp.log2(mass)
    rows = jnp.transpose(level)[0:8]
    left, right = split3(rows[:, :128]), split3(rows[:, 128:])
    at = lax.broadcasted_iota(jnp.int32, (8, 128), 0)
    tile = jnp.where(at == 0, left[0], 0.0)
    for r, part in enumerate((left[1], left[2], right[0], right[1], right[2])):
        tile = jnp.where(at == r + 1, part, tile)
    out_ref[256:272] = jnp.concatenate([tile, tile], axis=0).astype(jnp.bfloat16)


def rest_kernel(scale, nk, q_ref, peak_ref, weighted_ref, *refs):
    pieces = list(zip(refs[:nk], refs[nk : 2 * nk]))
    out_ref = refs[2 * nk]
    peak, weighted = attend(
        q_ref[...], pieces, scale, (peak_ref[:, 0:1], weighted_ref[...])
    )
    pack(peak, weighted, scale, out_ref)


def rest_call(query, state, keys, values, scale):
    nk = len(keys)
    return pl.pallas_call(
        functools.partial(rest_kernel, scale, nk),
        out_shape=jax.ShapeDtypeStruct((272, 128), jnp.bfloat16),
        in_specs=[VMEM] * (3 + 2 * nk),
        out_specs=VMEM,
        compiler_params=params(),
        name="rest_keys",
    )(query, *state, *keys, *values)


def level_row(part_ref):
    tile = part_ref[256:272].astype(jnp.float32)
    left = tile[0:1] + tile[1:2] + tile[2:3]
    right = tile[3:4] + tile[4:5] + tile[5:6]
    return jnp.concatenate([left, right], axis=1)


def merge_kernel(q_ref, ow_ref, *refs):
    parts, out_ref = refs[:-1], refs[-1]
    levels = [level_row(p) for p in parts]
    top = functools.reduce(jnp.maximum, levels)
    gains = [jnp.exp2(v - top) for v in levels]
    total = functools.reduce(jnp.add, gains)
    at = lax.broadcasted_iota(jnp.int32, (128, 256), 0)
    rows = jnp.zeros((128, 256), jnp.float32)
    for i, g in enumerate(gains):
        rows = jnp.where(at == i, g / total, rows)
    cols = jnp.transpose(rows)
    message = jnp.zeros((256, 128), jnp.float32)
    for i, p in enumerate(parts):
        message = message + p[0:256].astype(jnp.float32) * cols[:, i : i + 1]
    mixed = q_ref[...].astype(jnp.float32) + jnp.dot(
        message.astype(jnp.bfloat16), ow_ref[...], preferred_element_type=jnp.float32
    )
    out_ref[...] = mixed.astype(jnp.bfloat16)


def merge_call(query, ow, parts):
    return pl.pallas_call(
        merge_kernel,
        out_shape=jax.ShapeDtypeStruct((256, 128), jnp.bfloat16),
        in_specs=[VMEM] * (2 + len(parts)),
        out_specs=VMEM,
        compiler_params=params(),
        name="merge",
    )(query, ow, *parts)


def conv_kernel(above_ref, here_ref, below_ref, w_ref, bias_ref, out_ref):
    total = jnp.zeros((256, 384), jnp.float32)
    for a, row in enumerate((above_ref, here_ref, below_ref)):
        taps = jnp.concatenate([w_ref[a, b] for b in range(3)], axis=1)
        total = total + jnp.dot(row[...], taps, preferred_element_type=jnp.float32)
    at = lax.broadcasted_iota(jnp.int32, (256, 128), 0)
    left = jnp.where(at == 0, 0.0, pltpu.roll(total[:, 0:128], 1, 0))
    right = jnp.where(at == 255, 0.0, pltpu.roll(total[:, 256:384], 255, 0))
    conv = left + total[:, 128:256] + right + bias_ref[...].astype(jnp.float32)
    out_ref[...] = (here_ref[...].astype(jnp.float32) + jax.nn.gelu(conv)).astype(jnp.bfloat16)


def conv_call(above, here, below, w, bias):
    return pl.pallas_call(
        conv_kernel,
        out_shape=jax.ShapeDtypeStruct((256, 128), jnp.bfloat16),
        in_specs=[VMEM] * 5,
        out_specs=VMEM,
        compiler_params=params(),
        name="refine",
    )(above, here, below, w, bias.reshape(1, 128))


def local(feat_first, feat_second, value_weight, out_weight, conv_weight, conv_bias):
    scale = feat_first.shape[1] ** -0.5 * LOG2E
    near = [send(feat_second, x=s) for s in (1, 3, 2)]
    queries = [feat_first] + [send(feat_first, y=s) for s in (1, 2, 3)]
    mine = jnp.concatenate([feat_second] + near, axis=0)
    far = [send(mine, z=s) for s in (1, 3, 2)]
    other = send(mine, c=1)
    state = first_call(queries, [mine, other], value_weight, scale)
    keys = far + [send(block, c=1) for block in far]
    values = values_call(keys, value_weight)
    parts = []
    for i in (1, 2, 3, 0):
        part = rest_call(queries[i], state[i], keys, values, scale)
        parts.append(send(part, y=-i) if i else part)
    mixed = merge_call(feat_first, out_weight, parts)
    below_to_above = lax.ppermute(mixed, AXES, [(i, i + 1) for i in range(127)])
    above_to_below = lax.ppermute(mixed, AXES, [(i + 1, i) for i in range(127)])
    refined = conv_call(below_to_above, mixed, above_to_below, conv_weight, conv_bias)
    return refined.reshape(1, 256, 128)


def solution(mesh):
    in_specs = (P(("pb", "ka"), None), P(("ka", "pb"), None), P(), P(), P(), P())
    out_specs = P(("pb", "ka"), None, None)
    return jax.shard_map(local, mesh=mesh, in_specs=in_specs, out_specs=out_specs, check_vma=False)
```

time: 426 us -> 75.3 us (0.18)
  blocking collectives: 132 us -> 0 us
  waiting for transfers between devices: 146 us -> 31.2 us
  other arithmetic: 71.8 us -> 0 us
  local copies, waits for them, and re-layouts: 26.5 us -> 0.94 us
  matrix products: 23 us -> 0 us
  Pallas kernels: 0 us -> 18.7 us
  starting transfers between devices: 9.4 us -> 24.1 us
  between operations: 13.8 us -> 0.13 us
    all_gather x2 -> x0, waiting for transfers between devices: 136 us -> none  [the longest x1 136 us: joined(): pieces = jax.tree.map(lambda part: lax.all_gather(part, axis), value)]
    all_gather x4 -> x0, blocking collectives: 109 us -> none  [the longest x2 38.5 us: joined(): pieces = jax.tree.map(lambda part: lax.all_gather(part, axis), value)]
    add x34 -> x0, other arithmetic: 63 us -> none  [the longest x15 62.5 us: combine_parts(): earlier[2] * early_factor[:, None] + later[2] * late_factor[:, None]]
    all_to_all x2 -> x0, blocking collectives: 23.6 us -> none  [the longest x1 13.6 us: local(): lax.all_to_all(result, 'ka', split_axis=0, concat_axis=1, tiled=True)]
    dot_general x19 -> x0, matrix products: 23 us -> none  [the longest x4 11.4 us: update(): jnp.dot(expo.astype(jnp.bfloat16), values_part, preferred_element_type=jn...]
    slice x7 -> x0, local copies, waits for them, and re-layouts: 21.9 us -> none  [the longest x3 21.8 us: joined(): tail = jax.tree.map(lambda part: part[1:], pieces)]
    ppermute x4 -> x18, waiting for transfers between devices: 9.52 us -> 31.2 us  [the longest x16 25.1 us: send(): return lax.ppermute(block, AXES, pairs)]
    pallas_call x0 -> x8, Pallas kernels: none -> 18.7 us  [the longest x4 13.7 us: rest_call(): pl.pallas_call(functools.partial(rest_kernel, scale, nk), out_shape=jax.S...]
  transfers between devices with their start and end apart: 6 -> 18, of which waited for: 3 -> 9; matrix products, arithmetic and copies ran while one was open for 0% -> 1% of each run, Pallas kernels for 0% -> 18%
where the time goes in v1:
time: 75.3 us; the launch traced here: 75.1 us
  waiting for transfers between devices  31.2 us (41%)
  starting transfers between devices  24.1 us (32%)
  Pallas kernels  18.7 us (25%)
  local copies, waits for them, and re-layouts  0.94 us (1%)
    ppermute x16, waiting for transfers between devices, send(): return lax.ppermute(block, AXES, pairs)  25.1 us
    ppermute x16, starting transfers between devices, send(): return lax.ppermute(block, AXES, pairs)  19.6 us
    pallas_call x4, Pallas kernels, rest_call(): pl.pallas_call(functools.partial(rest_kernel, scale, nk), out_shape=jax.S...  13.7 us
    ppermute x1, waiting for transfers between devices, local(): below_to_above = lax.ppermute(mixed, AXES, [(i, i + 1) for i in range(127)])  6.17 us
    pallas_call x1, Pallas kernels, first_call(): pl.pallas_call(functools.partial(first_kernel, scale, nq, nk), out_shape=...  2.93 us
    ppermute x1, starting transfers between devices, local(): below_to_above = lax.ppermute(mixed, AXES, [(i, i + 1) for i in range(127)])  2.41 us
    ppermute x1, starting transfers between devices, local(): above_to_below = lax.ppermute(mixed, AXES, [(i + 1, i) for i in range(127)])  2.05 us
  transfers between devices with their start and end apart: 18, of which 9 were waited for; matrix products, arithmetic and copies ran while one was open for 1% of the time, Pallas kernels for 18%

profile of v1, /device:TPU:6, one launch (start us, length us, event | category | flops | bytes accessed | tf_op | source)
XLA Modules:
  0.0 75.1 jit_solution(488276856154231846)
XLA Ops:
  0.8 2.4 %collective-permute-start.3 = (bf16[256,128]{1,0:T(8,128)(2,1)}, bf16[256,128]{1,0:T(8,128)(2,1)S(1)}, u32[]{:S(2)}, u32[]{:S(2)}) collective-permute-start(bf16[256,128]{1,0:T(8,128)(2,1)} %param.7), channel_id=1, source_target_pairs={{0,16},{1,17},{2,18},{3,19},{4,20},{5,21},{6,22},{7,23},{8,24},{9,... | collective-permute-start | bytes 196616 | tf_op jit(solution)/shard_map/ppermute | solution.py:42
  4.3 1.8 %collective-permute-done.3 = bf16[256,128]{1,0:T(8,128)(2,1)S(1)} collective-permute-done((bf16[256,128]{1,0:T(8,128)(2,1)}, bf16[256,128]{1,0:T(8,128)(2,1)S(1)}, u32[]{:S(2)}, u32[]{:S(2)}) %collective-permute-start.3) | collective-permute-done | bytes 65568 | tf_op jit(solution)/shard_map/ppermute | solution.py:42
  6.2 3.0 %collective-permute-done.5 = bf16[256,128]{1,0:T(8,128)(2,1)S(1)} collective-permute-done((bf16[256,128]{1,0:T(8,128)(2,1)}, bf16[256,128]{1,0:T(8,128)(2,1)S(1)}, u32[]{:S(2)}, u32[]{:S(2)}) %collective-permute-start.5) | collective-permute-done | bytes 65568 | tf_op jit(solution)/shard_map/ppermute | solution.py:42
  9.2 4.0 %collective-permute-start.9 = (bf16[1024,128]{1,0:T(8,128)(2,1)S(1)}, bf16[1024,128]{1,0:T(8,128)(2,1)S(1)}, u32[]{:S(2)}, u32[]{:S(2)}) collective-permute-start(bf16[1024,128]{1,0:T(8,128)(2,1)S(1)} %constant_dynamic-update-slice_fusion.refs_4_), channel_id=1, source_target_pairs={{0,64},{1,65},{2,66},{3,67},{4,68},{5,69},{6,70},{7,71},{8,72},{9,... | collective-permute-start | bytes 786440 | tf_op jit(solution)/shard_map/ppermute | solution.py:42
  13.9 1.3 %collective-permute-start.7 = (bf16[1024,128]{1,0:T(8,128)(2,1)S(1)}, bf16[1024,128]{1,0:T(8,128)(2,1)S(1)}, u32[]{:S(2)}, u32[]{:S(2)}) collective-permute-start(bf16[1024,128]{1,0:T(8,128)(2,1)S(1)} %constant_dynamic-update-slice_fusion.refs_4_), channel_id=1, source_target_pairs={{0,8},{1,9},{2,10},{3,11},{4,12},{5,13},{6,14},{7,15},{8,64},{9,65... | collective-permute-start | bytes 786440 | tf_op jit(solution)/shard_map/ppermute | solution.py:42
  15.2 5.1 %collective-permute-done.9.refs_2_ = bf16[1024,128]{1,0:T(8,128)(2,1)S(1)} collective-permute-done((bf16[1024,128]{1,0:T(8,128)(2,1)S(1)}, bf16[1024,128]{1,0:T(8,128)(2,1)S(1)}, u32[]{:S(2)}, u32[]{:S(2)}) %collective-permute-start.9) | collective-permute-done | bytes 262176 | tf_op jit(solution)/shard_map/ppermute | solution.py:42
  20.4 3.8 %collective-permute-done.8.refs_1_ = bf16[1024,128]{1,0:T(8,128)(2,1)S(1)} collective-permute-done((bf16[1024,128]{1,0:T(8,128)(2,1)S(1)}, bf16[1024,128]{1,0:T(8,128)(2,1)S(1)}, u32[]{:S(2)}, u32[]{:S(2)}) %collective-permute-start.8) | collective-permute-done | bytes 262176 | tf_op jit(solution)/shard_map/ppermute | solution.py:42
  24.7 3.0 %collective-permute-start.2 = (bf16[256,128]{1,0:T(8,128)(2,1)S(1)}, bf16[256,128]{1,0:T(8,128)(2,1)S(1)}, u32[]{:S(2)}, u32[]{:S(2)}) collective-permute-start(bf16[256,128]{1,0:T(8,128)(2,1)S(1)} %copy-done), channel_id=1, source_target_pairs={{0,6},{1,7},{2,0},{3,1},{4,2},{5,3},{6,4},{7,5},{8,14},{9,15},{10,... | collective-permute-start | bytes 196616 | tf_op jit(solution)/shard_map/ppermute | solution.py:42
  27.7 1.9 %collective-permute-done.2.refs_3_.q_ref = bf16[256,128]{1,0:T(8,128)(2,1)S(1)} collective-permute-done((bf16[256,128]{1,0:T(8,128)(2,1)S(1)}, bf16[256,128]{1,0:T(8,128)(2,1)S(1)}, u32[]{:S(2)}, u32[]{:S(2)}) %collective-permute-start.2) | collective-permute-done | bytes 65568 | tf_op jit(solution)/shard_map/ppermute | solution.py:42
  29.6 2.5 %collective-permute-start.1 = (bf16[256,128]{1,0:T(8,128)(2,1)S(1)}, bf16[256,128]{1,0:T(8,128)(2,1)S(1)}, u32[]{:S(2)}, u32[]{:S(2)}) collective-permute-start(bf16[256,128]{1,0:T(8,128)(2,1)S(1)} %copy-done), channel_id=1, source_target_pairs={{0,4},{1,5},{2,6},{3,7},{4,0},{5,1},{6,2},{7,3},{8,12},{9,13},{10,... | collective-permute-start | bytes 196616 | tf_op jit(solution)/shard_map/ppermute | solution.py:42
  32.2 3.2 %collective-permute-done.1.refs_2_.q_ref = bf16[256,128]{1,0:T(8,128)(2,1)S(1)} collective-permute-done((bf16[256,128]{1,0:T(8,128)(2,1)S(1)}, bf16[256,128]{1,0:T(8,128)(2,1)S(1)}, u32[]{:S(2)}, u32[]{:S(2)}) %collective-permute-start.1) | collective-permute-done | bytes 65568 | tf_op jit(solution)/shard_map/ppermute | solution.py:42
  35.4 0.9 %collective-permute-start = (bf16[256,128]{1,0:T(8,128)(2,1)S(1)}, bf16[256,128]{1,0:T(8,128)(2,1)S(1)}, u32[]{:S(2)}, u32[]{:S(2)}) collective-permute-start(bf16[256,128]{1,0:T(8,128)(2,1)S(1)} %copy-done), channel_id=1, source_target_pairs={{0,2},{1,3},{2,4},{3,5},{4,6},{5,7},{6,0},{7,1},{8,10},{9,11},{10,... | collective-permute-start | bytes 196616 | tf_op jit(solution)/shard_map/ppermute | solution.py:42
  36.3 4.9 %collective-permute-done.refs_1_.q_ref = bf16[256,128]{1,0:T(8,128)(2,1)S(1)} collective-permute-done((bf16[256,128]{1,0:T(8,128)(2,1)S(1)}, bf16[256,128]{1,0:T(8,128)(2,1)S(1)}, u32[]{:S(2)}, u32[]{:S(2)}) %collective-permute-start) | collective-permute-done | bytes 65568 | tf_op jit(solution)/shard_map/ppermute | solution.py:42
  41.2 2.9 %first_keys.1 = (f32[256,128]{1,0:T(8,128)S(1)}, f32[256,256]{1,0:T(8,128)S(1)}, f32[256,128]{1,0:T(8,128)S(1)}, f32[256,256]{1,0:T(8,128)S(1)}, f32[256,128]{1,...) custom-call(bf16[256,128]{1,0:T(8,128)(2,1)S(1)} %copy-done, ...), custom_call_target="tpu_custom_call" | custom-call | tf_op jit(solution)/shard_map/first_keys/pallas_call | solution.py:96
  44.7 3.4 %rest_keys.4 = bf16[272,128]{1,0:T(8,128)(2,1)S(1)} custom-call(bf16[256,128]{1,0:T(8,128)(2,1)S(1)} %collective-permute-done.refs_1_.q_ref, f32[256,128]{1,0:T(8,128)S(1)} %get-tuple-element.19.peak_ref, f32[256,256]{1,0:T(8,128)S(1)} %get-tuple-element.20.weighted_ref, bf16[1024,128]{1,0:T(8,128)(2,1)S(1)} %collective-permute-done.7.refs_0_, ...), custom_call_target="tpu_custom_call" | custom-call | tf_op jit(solution)/shard_map/rest_keys/pallas_call | solution.py:155
  48.2 2.2 %collective-permute-start.13 = (bf16[272,128]{1,0:T(8,128)(2,1)S(1)}, bf16[272,128]{1,0:T(8,128)(2,1)S(1)}, u32[]{:S(2)}, u32[]{:S(2)}) collective-permute-start(bf16[272,128]{1,0:T(8,128)(2,1)S(1)} %rest_keys.4), channel_id=1, source_target_pairs={{0,6},{1,7},{2,0},{3,1},{4,2},{5,3},{6,4},{7,5},{8,14},{9,15},{10,... | collective-permute-start | bytes 208904 | tf_op jit(solution)/shard_map/ppermute | solution.py:42
  50.4 3.4 %rest_keys.5 = bf16[272,128]{1,0:T(8,128)(2,1)S(1)} custom-call(bf16[256,128]{1,0:T(8,128)(2,1)S(1)} %collective-permute-done.1.refs_2_.q_ref, f32[256,128]{1,0:T(8,128)S(1)} %get-tuple-element.27.peak_ref, f32[256,256]{1,0:T(8,128)S(1)} %get-tuple-element.28.weighted_ref, bf16[1024,128]{1,0:T(8,128)(2,1)S(1)} %collective-permute-done.7.refs_0_, ...), custom_call_target="tpu_custom_call" | custom-call | tf_op jit(solution)/shard_map/rest_keys/pallas_call | solution.py:155
  53.9 3.4 %rest_keys.6 = bf16[272,128]{1,0:T(8,128)(2,1)S(1)} custom-call(bf16[256,128]{1,0:T(8,128)(2,1)S(1)} %collective-permute-done.2.refs_3_.q_ref, f32[256,128]{1,0:T(8,128)S(1)} %get-tuple-element.29.peak_ref, f32[256,256]{1,0:T(8,128)S(1)} %get-tuple-element.30.weighted_ref, bf16[1024,128]{1,0:T(8,128)(2,1)S(1)} %collective-permute-done.7.refs_0_, ...), custom_call_target="tpu_custom_call" | custom-call | tf_op jit(solution)/shard_map/rest_keys/pallas_call | solution.py:155
  58.2 3.4 %rest_keys.7.refs_3_ = bf16[272,128]{1,0:T(8,128)(2,1)S(1)} custom-call(bf16[256,128]{1,0:T(8,128)(2,1)S(1)} %copy-done, f32[256,128]{1,0:T(8,128)S(1)} %get-tuple-element.31.peak_ref, f32[256,256]{1,0:T(8,128)S(1)} %get-tuple-element.32.weighted_ref, bf16[1024,128]{1,0:T(8,128)(2,1)S(1)} %collective-permute-done.7.refs_0_, ...), custom_call_target="tpu_custom_call" | custom-call | tf_op jit(solution)/shard_map/rest_keys/pallas_call | solution.py:155
  61.6 1.2 %collective-permute-done.15.refs_2_ = bf16[272,128]{1,0:T(8,128)(2,1)S(1)} collective-permute-done((bf16[272,128]{1,0:T(8,128)(2,1)S(1)}, bf16[272,128]{1,0:T(8,128)(2,1)S(1)}, u32[]{:S(2)}, u32[]{:S(2)}) %collective-permute-start.15) | collective-permute-done | bytes 69664 | tf_op jit(solution)/shard_map/ppermute | solution.py:42
  63.4 2.1 %collective-permute-start.17 = (bf16[256,128]{1,0:T(8,128)(2,1)S(1)}, bf16[256,128]{1,0:T(8,128)(2,1)S(1)}, u32[]{:S(2)}, u32[]{:S(2)}) collective-permute-start(bf16[256,128]{1,0:T(8,128)(2,1)S(1)} %merge.1.here_ref), channel_id=1, source_target_pairs={{1,0},{2,1},{3,2},{4,3},{5,4},{6,5},{7,6},{8,7},{9,8},{10,9},{11,1... | collective-permute-start | bytes 196616 | tf_op jit(solution)/shard_map/ppermute | solution.py:242
  65.5 2.4 %collective-permute-start.16 = (bf16[256,128]{1,0:T(8,128)(2,1)S(1)}, bf16[256,128]{1,0:T(8,128)(2,1)S(1)}, u32[]{:S(2)}, u32[]{:S(2)}) collective-permute-start(bf16[256,128]{1,0:T(8,128)(2,1)S(1)} %merge.1.here_ref), channel_id=1, source_target_pairs={{0,1},{1,2},{2,3},{3,4},{4,5},{5,6},{6,7},{7,8},{8,9},{9,10},{10,1... | collective-permute-start | bytes 196616 | tf_op jit(solution)/shard_map/ppermute | solution.py:241
  67.9 6.2 %collective-permute-done.16.above_ref = bf16[256,128]{1,0:T(8,128)(2,1)S(1)} collective-permute-done((bf16[256,128]{1,0:T(8,128)(2,1)S(1)}, bf16[256,128]{1,0:T(8,128)(2,1)S(1)}, u32[]{:S(2)}, u32[]{:S(2)}) %collective-permute-start.16) | collective-permute-done | bytes 65568 | tf_op jit(solution)/shard_map/ppermute | solution.py:241
  74.1 1.0 %refine.1 = bf16[256,128]{1,0:T(8,128)(2,1)} custom-call(bf16[256,128]{1,0:T(8,128)(2,1)S(1)} %collective-permute-done.16.above_ref, bf16[256,128]{1,0:T(8,128)(2,1)S(1)} %merge.1.here_ref, bf16[256,128]{1,0:T(8,128)(2,1)S(1)} %collective-permute-done.17.below_ref, bf16[3,3,128,128]{3,2,1,0:T(8,128)(2,1)S(1)} %copy-done.1, bf16[1,128]{1,0:T(2,128)(2,1)S(1)} %bitcast.2), custom_call_target="tpu_custom_call" | custom-call | tf_op jit(solution)/shard_map/refine/pallas_call | solution.py:216
  (34 shorter events, 5.3 us)
Async XLA Ops:
  0.0 6.1 %collective-permute-start.4 = (bf16[256,128]{1,0:T(8,128)(2,1)}, bf16[256,128]{1,0:T(8,128)(2,1)S(1)}, u32[]{:S(2)}, u32[]{:S(2)}) collective-permute-start(bf16[256,128]{1,0:T(8,128)(2,1)} %param.7), channel_id=1, source_target_pairs={{0,48},{1,49},{2,50},{3,51},{4,52},{5,53},{6,54},{7,55},{8,56},{9,... | collective-permute-start | bytes 196616 | tf_op jit(solution)/shard_map/ppermute | solution.py:42
  0.8 5.3 %collective-permute-start.3 = (bf16[256,128]{1,0:T(8,128)(2,1)}, bf16[256,128]{1,0:T(8,128)(2,1)S(1)}, u32[]{:S(2)}, u32[]{:S(2)}) collective-permute-start(bf16[256,128]{1,0:T(8,128)(2,1)} %param.7), channel_id=1, source_target_pairs={{0,16},{1,17},{2,18},{3,19},{4,20},{5,21},{6,22},{7,23},{8,24},{9,... | collective-permute-start | bytes 196616 | tf_op jit(solution)/shard_map/ppermute | solution.py:42
  3.2 6.0 %collective-permute-start.5 = (bf16[256,128]{1,0:T(8,128)(2,1)}, bf16[256,128]{1,0:T(8,128)(2,1)S(1)}, u32[]{:S(2)}, u32[]{:S(2)}) collective-permute-start(bf16[256,128]{1,0:T(8,128)(2,1)} %param.7), channel_id=1, source_target_pairs={{0,32},{1,33},{2,34},{3,35},{4,36},{5,37},{6,38},{7,39},{8,40},{9,... | collective-permute-start | bytes 196616 | tf_op jit(solution)/shard_map/ppermute | solution.py:42
  6.2 18.5 %copy-start = (bf16[256,128]{1,0:T(8,128)(2,1)S(1)}, bf16[256,128]{1,0:T(8,128)(2,1)}, u32[]{:S(2)}) copy-start(bf16[256,128]{1,0:T(8,128)(2,1)} %q_ref.3) | copy-start | bytes 196612
  6.2 35.0 %copy-start.2 = (bf16[128,128]{1,0:T(8,128)(2,1)S(1)}, bf16[128,128]{1,0:T(8,128)(2,1)}, u32[]{:S(2)}) copy-start(bf16[128,128]{1,0:T(8,128)(2,1)} %refs_6_.3) | copy-start | bytes 98308
  9.2 11.1 %collective-permute-start.9 = (bf16[1024,128]{1,0:T(8,128)(2,1)S(1)}, bf16[1024,128]{1,0:T(8,128)(2,1)S(1)}, u32[]{:S(2)}, u32[]{:S(2)}) collective-permute-start(bf16[1024,128]{1,0:T(8,128)(2,1)S(1)} %constant_dynamic-update-slice_fusion.refs_4_), channel_id=1, source_target_pairs={{0,64},{1,65},{2,66},{3,67},{4,68},{5,69},{6,70},{7,71},{8,72},{9,... | collective-permute-start | bytes 786440 | tf_op jit(solution)/shard_map/ppermute | solution.py:42
  13.2 11.0 %collective-permute-start.8 = (bf16[1024,128]{1,0:T(8,128)(2,1)S(1)}, bf16[1024,128]{1,0:T(8,128)(2,1)S(1)}, u32[]{:S(2)}, u32[]{:S(2)}) collective-permute-start(bf16[1024,128]{1,0:T(8,128)(2,1)S(1)} %constant_dynamic-update-slice_fusion.refs_4_), channel_id=1, source_target_pairs={{0,72},{1,73},{2,74},{3,75},{4,76},{5,77},{6,78},{7,79},{8,0},{9,1... | collective-permute-start | bytes 786440 | tf_op jit(solution)/shard_map/ppermute | solution.py:42
  13.9 10.3 %collective-permute-start.7 = (bf16[1024,128]{1,0:T(8,128)(2,1)S(1)}, bf16[1024,128]{1,0:T(8,128)(2,1)S(1)}, u32[]{:S(2)}, u32[]{:S(2)}) collective-permute-start(bf16[1024,128]{1,0:T(8,128)(2,1)S(1)} %constant_dynamic-update-slice_fusion.refs_4_), channel_id=1, source_target_pairs={{0,8},{1,9},{2,10},{3,11},{4,12},{5,13},{6,14},{7,15},{8,64},{9,65... | collective-permute-start | bytes 786440 | tf_op jit(solution)/shard_map/ppermute | solution.py:42
  15.2 26.0 %collective-permute-start.6 = (bf16[1024,128]{1,0:T(8,128)(2,1)S(1)}, bf16[1024,128]{1,0:T(8,128)(2,1)S(1)}, u32[]{:S(2)}, u32[]{:S(2)}) collective-permute-start(bf16[1024,128]{1,0:T(8,128)(2,1)S(1)} %constant_dynamic-update-slice_fusion.refs_4_), channel_id=1, source_target_pairs={{0,1},{1,0},{2,3},{3,2},{4,5},{5,4},{6,7},{7,6},{8,9},{9,8},{10,11... | collective-permute-start | bytes 786440 | tf_op jit(solution)/shard_map/ppermute | solution.py:42
  20.3 23.8 %collective-permute-start.12 = (bf16[1024,128]{1,0:T(8,128)(2,1)S(1)}, bf16[1024,128]{1,0:T(8,128)(2,1)S(1)}, u32[]{:S(2)}, u32[]{:S(2)}) collective-permute-start(bf16[1024,128]{1,0:T(8,128)(2,1)S(1)} %collective-permute-done.9.refs_2_), channel_id=1, source_target_pairs={{0,1},{1,0},{2,3},{3,2},{4,5},{5,4},{6,7},{7,6},{8,9},{9,8},{10,11... | collective-permute-start | bytes 786440 | tf_op jit(solution)/shard_map/ppermute | solution.py:42
  24.2 20.0 %collective-permute-start.11 = (bf16[1024,128]{1,0:T(8,128)(2,1)S(1)}, bf16[1024,128]{1,0:T(8,128)(2,1)S(1)}, u32[]{:S(2)}, u32[]{:S(2)}) collective-permute-start(bf16[1024,128]{1,0:T(8,128)(2,1)S(1)} %collective-permute-done.8.refs_1_), channel_id=1, source_target_pairs={{0,1},{1,0},{2,3},{3,2},{4,5},{5,4},{6,7},{7,6},{8,9},{9,8},{10,11... | collective-permute-start | bytes 786440 | tf_op jit(solution)/shard_map/ppermute | solution.py:42
  24.2 20.0 %collective-permute-start.10 = (bf16[1024,128]{1,0:T(8,128)(2,1)S(1)}, bf16[1024,128]{1,0:T(8,128)(2,1)S(1)}, u32[]{:S(2)}, u32[]{:S(2)}) collective-permute-start(bf16[1024,128]{1,0:T(8,128)(2,1)S(1)} %collective-permute-done.7.refs_0_), channel_id=1, source_target_pairs={{0,1},{1,0},{2,3},{3,2},{4,5},{5,4},{6,7},{7,6},{8,9},{9,8},{10,11... | collective-permute-start | bytes 786440 | tf_op jit(solution)/shard_map/ppermute | solution.py:42
  24.7 4.9 %collective-permute-start.2 = (bf16[256,128]{1,0:T(8,128)(2,1)S(1)}, bf16[256,128]{1,0:T(8,128)(2,1)S(1)}, u32[]{:S(2)}, u32[]{:S(2)}) collective-permute-start(bf16[256,128]{1,0:T(8,128)(2,1)S(1)} %copy-done), channel_id=1, source_target_pairs={{0,6},{1,7},{2,0},{3,1},{4,2},{5,3},{6,4},{7,5},{8,14},{9,15},{10,... | collective-permute-start | bytes 196616 | tf_op jit(solution)/shard_map/ppermute | solution.py:42
  29.6 5.8 %collective-permute-start.1 = (bf16[256,128]{1,0:T(8,128)(2,1)S(1)}, bf16[256,128]{1,0:T(8,128)(2,1)S(1)}, u32[]{:S(2)}, u32[]{:S(2)}) collective-permute-start(bf16[256,128]{1,0:T(8,128)(2,1)S(1)} %copy-done), channel_id=1, source_target_pairs={{0,4},{1,5},{2,6},{3,7},{4,0},{5,1},{6,2},{7,3},{8,12},{9,13},{10,... | collective-permute-start | bytes 196616 | tf_op jit(solution)/shard_map/ppermute | solution.py:42
  35.4 5.8 %collective-permute-start = (bf16[256,128]{1,0:T(8,128)(2,1)S(1)}, bf16[256,128]{1,0:T(8,128)(2,1)S(1)}, u32[]{:S(2)}, u32[]{:S(2)}) collective-permute-start(bf16[256,128]{1,0:T(8,128)(2,1)S(1)} %copy-done), channel_id=1, source_target_pairs={{0,2},{1,3},{2,4},{3,5},{4,6},{5,7},{6,0},{7,1},{8,10},{9,11},{10,... | collective-permute-start | bytes 196616 | tf_op jit(solution)/shard_map/ppermute | solution.py:42
  48.2 13.5 %collective-permute-start.13 = (bf16[272,128]{1,0:T(8,128)(2,1)S(1)}, bf16[272,128]{1,0:T(8,128)(2,1)S(1)}, u32[]{:S(2)}, u32[]{:S(2)}) collective-permute-start(bf16[272,128]{1,0:T(8,128)(2,1)S(1)} %rest_keys.4), channel_id=1, source_target_pairs={{0,6},{1,7},{2,0},{3,1},{4,2},{5,3},{6,4},{7,5},{8,14},{9,15},{10,... | collective-permute-start | bytes 208904 | tf_op jit(solution)/shard_map/ppermute | solution.py:42
  53.8 7.8 %collective-permute-start.14 = (bf16[272,128]{1,0:T(8,128)(2,1)S(1)}, bf16[272,128]{1,0:T(8,128)(2,1)S(1)}, u32[]{:S(2)}, u32[]{:S(2)}) collective-permute-start(bf16[272,128]{1,0:T(8,128)(2,1)S(1)} %rest_keys.5), channel_id=1, source_target_pairs={{0,4},{1,5},{2,6},{3,7},{4,0},{5,1},{6,2},{7,3},{8,12},{9,13},{10,... | collective-permute-start | bytes 208904 | tf_op jit(solution)/shard_map/ppermute | solution.py:42
  57.3 5.6 %collective-permute-start.15 = (bf16[272,128]{1,0:T(8,128)(2,1)S(1)}, bf16[272,128]{1,0:T(8,128)(2,1)S(1)}, u32[]{:S(2)}, u32[]{:S(2)}) collective-permute-start(bf16[272,128]{1,0:T(8,128)(2,1)S(1)} %rest_keys.6), channel_id=1, source_target_pairs={{0,2},{1,3},{2,4},{3,5},{4,6},{5,7},{6,0},{7,1},{8,10},{9,11},{10,... | collective-permute-start | bytes 208904 | tf_op jit(solution)/shard_map/ppermute | solution.py:42
  58.2 4.7 %copy-start.3 = (bf16[128,128]{1,0:T(8,128)(2,1)S(1)}, bf16[128,128]{1,0:T(8,128)(2,1)}, u32[]{:S(2)}) copy-start(bf16[128,128]{1,0:T(8,128)(2,1)} %ow_ref.1) | copy-start | bytes 98308
  61.6 12.5 %copy-start.1 = (bf16[3,3,128,128]{3,2,1,0:T(8,128)(2,1)S(1)}, bf16[3,3,128,128]{3,2,1,0:T(8,128)(2,1)}, u32[]{:S(2)}) copy-start(bf16[3,3,128,128]{3,2,1,0:T(8,128)(2,1)} %w_ref.1) | copy-start | bytes 884740
  63.4 10.7 %copy-start.4 = (bf16[128]{0:T(256)(128)(2,1)S(1)}, bf16[128]{0:T(256)(128)(2,1)}, u32[]{:S(2)}) copy-start(bf16[128]{0:T(256)(128)(2,1)} %param.11) | copy-start | bytes 772
  63.4 4.5 %collective-permute-start.17 = (bf16[256,128]{1,0:T(8,128)(2,1)S(1)}, bf16[256,128]{1,0:T(8,128)(2,1)S(1)}, u32[]{:S(2)}, u32[]{:S(2)}) collective-permute-start(bf16[256,128]{1,0:T(8,128)(2,1)S(1)} %merge.1.here_ref), channel_id=1, source_target_pairs={{1,0},{2,1},{3,2},{4,3},{5,4},{6,5},{7,6},{8,7},{9,8},{10,9},{11,1... | collective-permute-start | bytes 196616 | tf_op jit(solution)/shard_map/ppermute | solution.py:242
  65.5 8.6 %collective-permute-start.16 = (bf16[256,128]{1,0:T(8,128)(2,1)S(1)}, bf16[256,128]{1,0:T(8,128)(2,1)S(1)}, u32[]{:S(2)}, u32[]{:S(2)}) collective-permute-start(bf16[256,128]{1,0:T(8,128)(2,1)S(1)} %merge.1.here_ref), channel_id=1, source_target_pairs={{0,1},{1,2},{2,3},{3,4},{4,5},{5,6},{6,7},{7,8},{8,9},{9,10},{10,1... | collective-permute-start | bytes 196616 | tf_op jit(solution)/shard_map/ppermute | solution.py:241
